TPU v7x, 256 devices: a whole 4x4x8 slice. The times are simulated.
256 devices in a mesh: ctx: 64 (over z, y, core), tp: 4 (over x).
Axes of the slice: x: 4, y: 4, z: 8, core: 2. Of those that a mesh axis runs over, the one named last changes fastest.
Arguments:
- projected: bfloat16 [8192, 4, 4640], P('ctx', 'tp'), may hold values from -6 to 6
- conv_weight: float32 [4, 4, 2560], P('tp'), may hold values from -3 to 3
- conv_bias: float32 [4, 2560], P('tp'), may hold values from -1.5 to 1.5
- step_bias: float32 [4, 32], P('tp'), may hold values from -1 to 0.5
- log_rates: float32 [4, 32], P('tp'), as said below
- norm_gain: float32 [4, 2048], P('tp'), may hold values from 0.1 to 1.9
- out_weight: bfloat16 [4, 2048, 4096], P('tp', 'ctx'), may hold values from -0.0625 to 0.0625
Outputs:
- mixed: bfloat16 [8192, 4096], P('ctx', 'tp')
Inputs may be any that keep to these rules, and one draw needn't show every extreme that they name: log_rates lies between log(0.3 / 8192) and log(1 / 25).
All inputs are finite; a program needn't handle non-finite values.
Results may differ from a plain program's by a relative error of at most 0.0058.
Values may be sent and summed in bfloat16 or wider, within the bound.
No kernel may reach another device: no remote copies, remote signals or barrier semaphores. Data moves between devices by JAX's collectives and lax.ppermute only.
A program may use at most 320 MiB of HBM per device.

v0:
```python
import jax
import jax.numpy as jnp
import numpy as np
from jax import lax
from jax.sharding import PartitionSpec as P

P_SIZE = 64
N = 256
KCONV = 4
SPAN = 128
GCH = 2048
GCONV = 2560
highest_precision = lax.Precision.HIGHEST


def from_behind(shard, axis, by):
    peers = lax.axis_size(axis)
    pairs = [(i, i + by) for i in range(peers) if 0 <= i + by < peers]
    return lax.ppermute(shard, axis, pairs)


def ssd_blocks(inputs_x, step_sizes, decay_rate, b_keys, c_keys, block_rows):
    row_count = inputs_x.shape[0]
    block_count = row_count // block_rows
    head_count = inputs_x.shape[1]
    head_width = inputs_x.shape[2]
    state_count = b_keys.shape[1]
    x_blocks = inputs_x.reshape(block_count, block_rows, head_count, head_width)
    step_blocks = step_sizes.reshape(block_count, block_rows, head_count)
    b_blocks = b_keys.reshape(block_count, block_rows, state_count)
    c_blocks = c_keys.reshape(block_count, block_rows, state_count)
    causal_mask = (jnp.arange(block_rows)[:, None] >= jnp.arange(block_rows)[None, :])[None]

    def advance(carried, pieces):
        x_block, step_block, b_block, c_block = pieces
        log_steps = step_block * decay_rate[None, :]
        running = jnp.cumsum(log_steps, axis=0)
        intersection = jnp.dot(c_block, b_block.T, preferred_element_type=jnp.float32)
        b_float = b_block.astype(jnp.float32)
        c_float = c_block.astype(jnp.float32)
        log_gaps = running.T[:, :, None] - running.T[:, None, :]
        factors = jnp.where(causal_mask, jnp.exp(jnp.where(causal_mask, log_gaps, 0.0)), 0.0)
        factors = factors * intersection[None] * step_block.T[:, None, :]
        within = jnp.einsum("hts,shp->thp", factors, x_block, precision=highest_precision)
        carried_part = (
            jnp.einsum("tn,hpn->thp", c_float, carried, precision=highest_precision)
            * jnp.exp(running)[:, :, None]
        )
        tail_weight = jnp.exp(running[-1][None, :] - running) * step_block
        weighted = x_block * tail_weight[:, :, None]
        updated = carried * jnp.exp(running[-1])[:, None, None] + jnp.einsum(
            "shp,sn->hpn", weighted, b_float, precision=highest_precision
        )
        return (updated, within + carried_part)

    initial = jnp.zeros((head_count, head_width, state_count), jnp.float32)
    final_state, outputs = lax.scan(advance, initial, (x_blocks, step_blocks, b_blocks, c_blocks))
    total_log = jnp.sum(step_sizes * decay_rate[None, :], axis=0)
    return (outputs.reshape(row_count, head_count, head_width), final_state, total_log)


def on_device(projected, conv_weight, conv_bias, step_bias, log_rates, norm_gain, out_weight):
    row_count = projected.shape[0]
    conv_input = projected[:, :, GCH : GCH + GCONV]
    rim_rows = from_behind(conv_input[row_count - (KCONV - 1) :], "ctx", 1)
    padded = jnp.concatenate([rim_rows, conv_input], axis=0).astype(jnp.float32)
    mixed_conv = conv_bias[None]
    for offset in range(KCONV):
        mixed_conv = mixed_conv + conv_weight[:, offset][None] * padded[offset : offset + row_count]
    activated = jax.nn.silu(mixed_conv).astype(jnp.bfloat16)
    values = activated[:, :, :GCH]
    key_rows = activated[:, :, GCH:]
    raw_steps = projected[:, :, GCH + GCONV :]
    decay_rate = -jnp.exp(log_rates)
    devices = lax.axis_size("ctx")
    shard_width = GCH // devices
    shard_heads = max(1, shard_width // P_SIZE)
    piece_width = shard_width // shard_heads
    head_table = (
        np.arange(devices)[:, None] * shard_width // P_SIZE + np.arange(shard_heads)[None, :]
    ).reshape(-1)
    spread_steps = jnp.take(raw_steps, jnp.asarray(head_table, jnp.int32), axis=2)
    local_values, local_steps = (
        lax.all_to_all(values, "ctx", split_axis=2, concat_axis=0, tiled=True),
        lax.all_to_all(spread_steps, "ctx", split_axis=2, concat_axis=0, tiled=True),
    )
    all_keys = lax.all_gather(key_rows, "ctx", axis=0, tiled=True)
    sequence = local_values.shape[0]
    first_head = lax.axis_index("ctx") * shard_width // P_SIZE
    bias_slice = lax.dynamic_slice_in_dim(step_bias[0], first_head, shard_heads)
    rate_slice = lax.dynamic_slice_in_dim(decay_rate[0], first_head, shard_heads)
    step_sizes = jax.nn.softplus(local_steps[:, 0].astype(jnp.float32) + bias_slice[None, :])
    outputs, final_state, total_log = ssd_blocks(
        local_values[:, 0].astype(jnp.float32).reshape(sequence, shard_heads, piece_width),
        step_sizes,
        rate_slice,
        all_keys[:, 0, :N],
        all_keys[:, 0, N:],
        4 * SPAN,
    )
    pieces_out = [outputs.reshape(sequence, shard_width).astype(jnp.bfloat16)]
    scanned = lax.all_to_all(
        jnp.stack(pieces_out, axis=1), "ctx", split_axis=0, concat_axis=2, tiled=True
    )
    gated = scanned.astype(jnp.float32) * jax.nn.silu(projected[:, :, :GCH].astype(jnp.float32))
    normed = (
        gated * lax.rsqrt(jnp.mean(gated * gated, axis=2, keepdims=True) + 1e-05) * norm_gain[None]
    ).astype(jnp.bfloat16)
    summed = jnp.einsum(
        "tgr,grd->td",
        normed,
        lax.all_gather(out_weight, "ctx", axis=1, tiled=True),
        preferred_element_type=jnp.float32,
    )
    shares = lax.psum_scatter(summed, "tp", scatter_dimension=1, tiled=True)
    return shares.astype(jnp.bfloat16)


def solution(mesh):
    return jax.shard_map(
        on_device,
        mesh=mesh,
        in_specs=(
            P("ctx", "tp", None),
            P("tp", None, None),
            P("tp", None),
            P("tp", None),
            P("tp", None),
            P("tp", None),
            P("tp", "ctx", None),
        ),
        out_specs=P("ctx", "tp"),
        check_vma=False,
    )
```

profile of v0, /device:TPU:1, one launch (start us, length us, event | category | flops | bytes accessed | tf_op | source)
XLA Modules:
  0.0 387.9 jit_solution(16653090227472884516)
XLA Ops:
  6.5 1.4 slice.62
  8.2 4.7 %collective-permute-start = (bf16[3,1,2560]{2,0,1:T(4,128)(2,1)S(1)}, bf16[3,1,2560]{2,0,1:T(4,128)(2,1)S(1)}, u32[]{:S(2)}, u32[]{:S(2)}) collective-permute-start(bf16[3,1,2560]{2,0,1:T(4,128)(2,1)S(1)} %copy.77), channel_id=1, source_target_pairs={{0,4},{4,8},{8,12},{12,16},{16,20},{20,24},{24,28},{28,32},{32,36}... | collective-permute-start | bytes 46088 | tf_op jit(solution)/shard_map/ppermute | solution.py:19
  16.9 13.5 %all-to-all-start = ((bf16[128,1,64]{0,1,2:T(2,128)(2,1)}), bf16[128,1,64]{0,1,2:T(2,128)(2,1)S(1)}, u32[]{:S(2)}, u32[]{:S(2)}) async-start(bf16[128,1,64]{0,1,2:T(2,128)(2,1)} %copy.66), calls=%async_computation | async-start | bytes 65536 | tf_op jit(solution)/shard_map/all_to_all | solution.py:85
  31.7 11.5 %reduce.12 = bf16[2048,128]{1,0:T(8,128)(2,1)S(1)} reduce(bf16[2048,1,128]{2,1,0:T(2,128)(2,1)S(1)} %bitcast.163, bf16[]{:T(256)} %broadcast.159), dimensions={1}, to_apply=%bitcast.98.reduce_sub_computation | reduce | bytes 1048578
  44.2 10.3 %all-to-all-start.1 = ((bf16[64,2,2048]{2,1,0:T(2,128)(2,1)}), bf16[64,2,2048]{2,1,0:T(2,128)(2,1)S(1)}, u32[]{:S(2)}, u32[]{:S(2)}) async-start(bf16[64,2,2048]{2,1,0:T(2,128)(2,1)} %reshape.445), calls=%async_computation.1 | async-start | bytes 1048576 | tf_op jit(solution)/shard_map/all_to_all | solution.py:84
  57.5 14.9 %all-to-all-done.1 = bf16[64,2,2048]{2,1,0:T(2,128)(2,1)S(1)} async-done(((bf16[64,2,2048]{2,1,0:T(2,128)(2,1)}), bf16[64,2,2048]{2,1,0:T(2,128)(2,1)S(1)}, u32[]{:S(2)}, u32[]{:S(2)}) %all-to-all-start.1) | async-done | bytes 524320 | tf_op jit(solution)/shard_map/all_to_all | solution.py:84
  74.1 2.7 copy.70
  76.8 26.9 %all-gather.3.cloned.1.call-done = bf16[8192,1,512]{2,0,1:T(8,128)(2,1)} async-done(((bf16[128,1,512]{2,0,1:T(8,128)(2,1)}), bf16[8192,1,512]{2,0,1:T(8,128)(2,1)}) %all-gather.3.cloned.1.call-update) | async-done | bytes 8388624 | tf_op jit(solution)/shard_map/all_gather | solution.py:87
  103.7 5.9 %fusion.41 = (bf16[8192,1,256]{2,0,1:T(8,128)(2,1)}, bf16[8192,1,256]{2,0,1:T(8,128)(2,1)}) fusion(bf16[8192,1,512]{2,0,1:T(8,128)(2,1)} %all-gather.3.cloned.1.call-done), kind=kLoop, calls=%fused_computation.76 | loop fusion | bytes 16777216 | tf_op jit(solution)/shard_map/slice | solution.py:98
  109.6 184.8 %while.14 = (s32[]{:T(128)}, f32[1,32,256]{2,1,0:T(8,128)S(1)}, bf16[16,512,1,32]{1,3,2,0:T(8,128)(2,1)S(1)}, f32[16,512,1]{1,0,2:T(8,128)S(1)}, f32[1]{0:T(128)...) while((s32[]{:T(128)}, f32[1,32,256]{2,1,0:T(8,128)S(1)}, ...), condition=%wide.region_3.4_spmd.clone.clone, body=%wide.region_0.0_spmd.clone.clone.sunk | while | flops 337266176 | bytes 4002620 | solution.py:57
  113.5 2.4 broadcast_multiply_fusion.2
  115.9 1.4 fusion.69
  119.7 1.3 fusion.67
  125.0 2.4 broadcast_multiply_fusion.2
  127.4 1.4 fusion.69
  131.3 1.3 fusion.67
  136.5 2.4 broadcast_multiply_fusion.2
  139.0 1.4 fusion.69
  148.1 2.4 broadcast_multiply_fusion.2
  150.5 1.4 fusion.69
  154.3 1.4 fusion.67
  159.7 2.5 broadcast_multiply_fusion.2
  162.1 1.4 fusion.69
  166.0 1.4 fusion.67
  171.3 2.4 broadcast_multiply_fusion.2
  173.7 1.4 fusion.69
  177.6 1.3 fusion.67
  182.8 2.4 broadcast_multiply_fusion.2
  185.3 1.4 fusion.69
  186.7 1.3 fusion.68
  189.2 1.3 fusion.67
  194.4 2.4 broadcast_multiply_fusion.2
  196.8 1.4 fusion.69
  198.2 1.4 fusion.68
  200.8 1.3 fusion.67
  206.0 2.4 broadcast_multiply_fusion.2
  208.4 1.4 fusion.69
  212.3 1.3 fusion.67
  217.5 2.4 broadcast_multiply_fusion.2
  220.0 1.4 fusion.69
  223.8 1.3 fusion.67
  229.1 2.4 broadcast_multiply_fusion.2
  231.5 1.4 fusion.69
  235.4 1.3 fusion.67
  240.6 2.4 broadcast_multiply_fusion.2
  243.0 1.4 fusion.69
  246.9 1.3 fusion.67
  252.1 2.4 broadcast_multiply_fusion.2
  254.6 1.4 fusion.69
  263.7 2.4 broadcast_multiply_fusion.2
  266.1 1.4 fusion.69
  275.2 2.4 broadcast_multiply_fusion.2
  277.6 1.4 fusion.69
  286.7 2.4 broadcast_multiply_fusion.2
  289.1 1.4 fusion.69
  294.4 1.7 reduce.13
  296.0 1.9 copy.81
  298.0 2.8 reshape.447
  300.8 23.8 %all_to_all.12 = bf16[64,2,2048]{2,1,0:T(2,128)(2,1)S(1)} all-to-all(bf16[64,2,2048]{2,1,0:T(2,128)(2,1)} %reshape.447), channel_id=1, replica_groups=mesh['ctx'=64,'tp'=4] {'ctx'}, dimensions={0} | all-to-all | bytes 1048576 | tf_op jit(solution)/shard_map/all_to_all | solution.py:102
  324.6 7.1 %reshape.448 = bf16[8192,1,32]{2,1,0:T(2,128)(2,1)} reshape(bf16[64,2,2048]{2,1,0:T(2,128)(2,1)S(1)} %all_to_all.12) | data formatting | bytes 1048576
  331.8 8.0 %copy.74 = bf16[8192,1,32]{0,2,1:T(8,128)(2,1)S(1)} copy(bf16[8192,1,32]{2,1,0:T(2,128)(2,1)} %reshape.448) | data formatting | bytes 1048576 | tf_op jit(solution)/shard_map/all_to_all | solution.py:102
  341.3 9.6 %fusion.25 = f32[128,4096]{1,0:T(8,128)} fusion(bf16[1,2048,4096]{2,1,0:T(8,128)(2,1)} %all-gather.5.cloned.1.call-done, f32[128,1,2048]{0,2,1:T(8,128)S(1)} %get-tuple-element.150, f32[2048]{0:T(1024)S(1)} %bitcast.173, f32[128]{0:T(128)S(1)} %add_rsqrt_fusion), kind=kOutput, calls=%fused_computation.38 | convolution fusion | flops 2148270080 | bytes 19931648 | tf_op jit(solution)/shard_map/tgr,grd->td/dot_general | solution.py:109
  350.9 28.7 %reduce-scatter.2.cloned.1.call-done = f32[128,1024]{1,0:T(8,128)} async-done(((f32[128,4096]{1,0:T(8,128)}), f32[128,1024]{1,0:T(8,128)}) %reduce-scatter.2.cloned.1.call-update) | async-done | bytes 524304 | tf_op jit(solution)/shard_map/reduce_scatter | solution.py:115
  379.6 1.8 convert_element_type.107
  (255 shorter events, 97.0 us)
Async XLA Ops:
  6.5 49.0 %copy-start = (f32[1,32]{1,0:T(1,128)S(1)}, f32[1,32]{1,0:T(1,128)}, u32[]{:S(2)}) copy-start(f32[1,32]{1,0:T(1,128)} %param.13) | copy-start | bytes 388
  6.5 6.4 %copy-start.5 = (f32[1,4,2560]{2,1,0:T(4,128)S(1)}, f32[1,4,2560]{2,1,0:T(4,128)}, u32[]{:S(2)}) copy-start(f32[1,4,2560]{2,1,0:T(4,128)} %param.11) | copy-start | bytes 122884
  6.5 6.5 %slice-start = ((bf16[128,1,4640]{0,2,1:T(8,128)(2,1)}), bf16[128,1,2560]{0,2,1:T(8,128)(2,1)S(1)}, s32[]{:S(2)}) async-start(bf16[128,1,4640]{0,2,1:T(8,128)(2,1)} %param.10), calls=%async_computation.7 | async-start | bytes 1310720 | tf_op jit(solution)/shard_map/slice | solution.py:64
  6.5 97.2 %all-gather.3.cloned.1.call-start = ((), (), s32[]{:S(2)}) async-start(), calls=%async_computation.4 | async-start | bytes 8519680 | tf_op jit(solution)/shard_map/all_gather | solution.py:87
  8.2 5.1 %copy-start.6 = (f32[1,2560]{1,0:T(1,128)S(1)}, f32[1,2560]{1,0:T(1,128)}, u32[]{:S(2)}) copy-start(f32[1,2560]{1,0:T(1,128)} %param.12) | copy-start | bytes 30724
  8.2 5.6 %collective-permute-start = (bf16[3,1,2560]{2,0,1:T(4,128)(2,1)S(1)}, bf16[3,1,2560]{2,0,1:T(4,128)(2,1)S(1)}, u32[]{:S(2)}, u32[]{:S(2)}) collective-permute-start(bf16[3,1,2560]{2,0,1:T(4,128)(2,1)S(1)} %copy.77), channel_id=1, source_target_pairs={{0,4},{4,8},{8,12},{12,16},{16,20},{20,24},{24,28},{28,32},{32,36}... | collective-permute-start | bytes 46088 | tf_op jit(solution)/shard_map/ppermute | solution.py:19
  14.0 1.6 copy-start.7
  14.0 1.6 copy-start.2
  16.9 27.3 %all-to-all-start = ((bf16[128,1,64]{0,1,2:T(2,128)(2,1)}), bf16[128,1,64]{0,1,2:T(2,128)(2,1)S(1)}, u32[]{:S(2)}, u32[]{:S(2)}) async-start(bf16[128,1,64]{0,1,2:T(2,128)(2,1)} %copy.66), calls=%async_computation | async-start | bytes 65536 | tf_op jit(solution)/shard_map/all_to_all | solution.py:85
  43.2 13.0 %copy-start.8 = (f32[1,32]{1,0:T(1,128)S(1)}, f32[1,32]{1,0:T(1,128)}, u32[]{:S(2)}) copy-start(f32[1,32]{1,0:T(1,128)} %param.14) | copy-start | bytes 388
  44.2 28.2 %all-to-all-start.1 = ((bf16[64,2,2048]{2,1,0:T(2,128)(2,1)}), bf16[64,2,2048]{2,1,0:T(2,128)(2,1)S(1)}, u32[]{:S(2)}, u32[]{:S(2)}) async-start(bf16[64,2,2048]{2,1,0:T(2,128)(2,1)} %reshape.445), calls=%async_computation.1 | async-start | bytes 1048576 | tf_op jit(solution)/shard_map/all_to_all | solution.py:84
  54.5 286.5 %all-gather.5.cloned.1.call-start = ((), (), s32[]{:S(2)}) async-start(), calls=%async_computation.5 | async-start | bytes 17039360 | tf_op jit(solution)/shard_map/all_gather | solution.py:112
  55.3 324.3 %reduce-scatter.2.cloned.1.call-start = ((), (), s32[]{:S(2)}) async-start(), calls=%async_computation.6 | async-start | bytes 2621440 | tf_op jit(solution)/shard_map/reduce_scatter | solution.py:115
  76.8 32.8 %copy-start.3 = (bf16[16,512,1,32]{1,3,2,0:T(8,128)(2,1)S(1)}, bf16[16,512,1,32]{1,3,2,0:T(8,128)(2,1)}, u32[]{:S(2)}) copy-start(bf16[16,512,1,32]{1,3,2,0:T(8,128)(2,1)} %custom-call.3) | copy-start | bytes 1572868
  340.6 0.7 copy-start.4
  350.9 30.5 %copy-start.1 = (f32[1,32]{1,0:T(1,128)S(1)}, f32[1,32]{1,0:T(1,128)}, u32[]{:S(2)}) copy-start(f32[1,32]{1,0:T(1,128)} %param.13) | copy-start | bytes 388
Sparse Core Ops, SparseCore 0:
  15.7 87.9 all-gather.2
  106.5 97.1 all-gather.4
  351.1 28.4 reduce-scatter.1
where the time goes:
time: 391 us; the launch traced here: 388 us
  matrix products  91.8 us (23%)
  other arithmetic  75.4 us (19%)
  waiting for transfers between devices  71.7 us (18%)
  local copies, waits for them, and re-layouts  60.7 us (16%)
  starting transfers between devices  28.7 us (7%)
  blocking collectives  23.8 us (6%)
  loops' own time  22.3 us (6%)
  between operations  13.4 us (3%)
    mul x16, other arithmetic, advance(): weighted = x_block * tail_weight[:, :, None]  38.7 us
    reduce_scatter x1, waiting for transfers between devices, on_device(): shares = lax.psum_scatter(summed, 'tp', scatter_dimension=1, tiled=True)  28.7 us
    all_gather x1, waiting for transfers between devices, on_device(): all_keys = lax.all_gather(key_rows, 'ctx', axis=0, tiled=True)  26.9 us
    all_to_all x1, blocking collectives, on_device(): lax.all_to_all(jnp.stack(pieces_out, axis=1), 'ctx', split_axis=0, concat...  23.8 us
    another operation x1, loops' own time, ssd_blocks(): lax.scan(advance, initial, (x_blocks, step_blocks, b_blocks, c_blocks))  22.3 us
    dot_general x16, matrix products, advance(): jnp.dot(c_block, b_block.T, preferred_element_type=jnp.float32)  22 us
    dot_general x16, matrix products, advance(): jnp.einsum('shp,sn->hpn', weighted, b_float, precision=highest_precision)  21.3 us
    dot_general x16, matrix products, advance(): jnp.einsum('tn,hpn->thp', c_float, carried, precision=highest_precision)  20.8 us
  transfers between devices with their start and end apart: 6, of which 4 were waited for; matrix products, arithmetic and copies ran while one was open for 55% of the time, Pallas kernels for 0%

commit v1 on v0

--- a/solution.py
+++ b/solution.py
@@ -84,7 +84,9 @@
         lax.all_to_all(values, "ctx", split_axis=2, concat_axis=0, tiled=True),
         lax.all_to_all(spread_steps, "ctx", split_axis=2, concat_axis=0, tiled=True),
     )
-    all_keys = lax.all_gather(key_rows, "ctx", axis=0, tiled=True)
+    all_keys = jnp.concatenate(
+        lax.all_to_all(jnp.stack([key_rows] * lax.axis_size("ctx")), "ctx", 0, 0), axis=0
+    )
     sequence = local_values.shape[0]
     first_head = lax.axis_index("ctx") * shard_width // P_SIZE
     bias_slice = lax.dynamic_slice_in_dim(step_bias[0], first_head, shard_heads)

time: 391 us -> 604 us (1.54)
  waiting for transfers between devices: 71.7 us -> 272 us
  starting transfers between devices: 28.7 us -> 35 us
    all_to_all x0 -> x1, waiting for transfers between devices: none -> 225 us  [on_device(): lax.all_to_all(jnp.stack([key_rows] * lax.axis_size('ctx')), 'ctx', 0, 0)]
    all_gather x1 -> x0, waiting for transfers between devices: 26.9 us -> none  [on_device(): all_keys = lax.all_gather(key_rows, 'ctx', axis=0, tiled=True)]
    all_to_all x0 -> x1, starting transfers between devices: none -> 6.04 us  [on_device(): lax.all_to_all(jnp.stack([key_rows] * lax.axis_size('ctx')), 'ctx', 0, 0)]
    unnamed x27 -> x23, local copies, waits for them, and re-layouts: 14.9 us -> 13.9 us
  transfers between devices with their start and end apart: 6 -> 6, of which waited for: 4 -> 4; matrix products, arithmetic and copies ran while one was open for 55% -> 35% of each run, Pallas kernels for 0% -> 0%
where the time goes in v1:
time: 604 us; the launch traced here: 601 us
  waiting for transfers between devices  272 us (45%)
  matrix products  91.5 us (15%)
  other arithmetic  75.2 us (12%)
  local copies, waits for them, and re-layouts  64.8 us (11%)
  starting transfers between devices  35 us (6%)
  blocking collectives  26.5 us (4%)
  loops' own time  22 us (4%)
  between operations  13.7 us (2%)
    all_to_all x1, waiting for transfers between devices, on_device(): lax.all_to_all(jnp.stack([key_rows] * lax.axis_size('ctx')), 'ctx', 0, 0)  225 us
    mul x16, other arithmetic, advance(): weighted = x_block * tail_weight[:, :, None]  38.6 us
    reduce_scatter x1, waiting for transfers between devices, on_device(): shares = lax.psum_scatter(summed, 'tp', scatter_dimension=1, tiled=True)  28.8 us
    all_to_all x1, blocking collectives, on_device(): lax.all_to_all(jnp.stack(pieces_out, axis=1), 'ctx', split_axis=0, concat...  26.5 us
    another operation x1, loops' own time, ssd_blocks(): lax.scan(advance, initial, (x_blocks, step_blocks, b_blocks, c_blocks))  22 us
    dot_general x16, matrix products, advance(): jnp.dot(c_block, b_block.T, preferred_element_type=jnp.float32)  22 us
    dot_general x16, matrix products, advance(): jnp.einsum('shp,sn->hpn', weighted, b_float, precision=highest_precision)  21.2 us
    dot_general x16, matrix products, advance(): jnp.einsum('tn,hpn->thp', c_float, carried, precision=highest_precision)  20.6 us
  transfers between devices with their start and end apart: 6, of which 4 were waited for; matrix products, arithmetic and copies ran while one was open for 35% of the time, Pallas kernels for 0%

profile of v1, /device:TPU:1, one launch (start us, length us, event | category | flops | bytes accessed | tf_op | source)
XLA Modules:
  0.0 601.1 jit_solution(12963521938681404211)
XLA Ops:
  9.2 13.2 %all-to-all-start = ((bf16[128,1,64]{0,1,2:T(2,128)(2,1)}), bf16[128,1,64]{0,1,2:T(2,128)(2,1)S(1)}, u32[]{:S(2)}, u32[]{:S(2)}) async-start(bf16[128,1,64]{0,1,2:T(2,128)(2,1)} %copy.62), calls=%async_computation | async-start | bytes 65536 | tf_op jit(solution)/shard_map/all_to_all | solution.py:85
  22.4 1.4 slice.64
  24.0 3.7 collective-permute-start
  31.0 11.5 %reduce.12 = bf16[2048,128]{1,0:T(8,128)(2,1)S(1)} reduce(bf16[2048,1,128]{2,1,0:T(2,128)(2,1)S(1)} %bitcast.166, bf16[]{:T(256)} %broadcast.162), dimensions={1}, to_apply=%bitcast.101.reduce_sub_computation | reduce | bytes 1048578
  43.4 11.9 %all-to-all-start.1 = ((bf16[64,2,2048]{2,1,0:T(2,128)(2,1)}), bf16[64,2,2048]{2,1,0:T(2,128)(2,1)S(1)}, u32[]{:S(2)}, u32[]{:S(2)}) async-start(bf16[64,2,2048]{2,1,0:T(2,128)(2,1)} %reshape.452), calls=%async_computation.1 | async-start | bytes 1048576 | tf_op jit(solution)/shard_map/all_to_all | solution.py:84
  55.3 17.7 %all-to-all-done.1 = bf16[64,2,2048]{2,1,0:T(2,128)(2,1)S(1)} async-done(((bf16[64,2,2048]{2,1,0:T(2,128)(2,1)}), bf16[64,2,2048]{2,1,0:T(2,128)(2,1)S(1)}, u32[]{:S(2)}, u32[]{:S(2)}) %all-to-all-start.1) | async-done | bytes 524320 | tf_op jit(solution)/shard_map/all_to_all | solution.py:84
  73.0 4.2 stack.2
  77.2 6.0 %all-to-all-start.2 = ((bf16[64,128,1,512]{3,1,2,0:T(8,128)(2,1)}), bf16[64,128,1,512]{3,1,2,0:T(8,128)(2,1)}, u32[]{:S(2)}, u32[]{:S(2)}) async-start(bf16[64,128,1,512]{3,1,2,0:T(8,128)(2,1)} %stack.2), calls=%async_computation.2 | async-start | bytes 16777216 | tf_op jit(solution)/shard_map/all_to_all | solution.py:88
  88.0 2.7 copy.66
  90.7 224.7 %all-to-all-done.2 = bf16[64,128,1,512]{3,1,2,0:T(8,128)(2,1)} async-done(((bf16[64,128,1,512]{3,1,2,0:T(8,128)(2,1)}), bf16[64,128,1,512]{3,1,2,0:T(8,128)(2,1)}, u32[]{:S(2)}, u32[]{:S(2)}) %all-to-all-start.2) | async-done | bytes 8388640 | tf_op jit(solution)/shard_map/all_to_all | solution.py:88
  315.4 5.7 fusion.41
  321.1 184.8 %while.14 = (s32[]{:T(128)}, f32[1,32,256]{2,1,0:T(8,128)S(1)}, bf16[16,512,1,32]{1,3,2,0:T(8,128)(2,1)S(1)}, f32[16,512,1]{1,0,2:T(8,128)S(1)}, f32[1]{0:T(128)...) while((s32[]{:T(128)}, f32[1,32,256]{2,1,0:T(8,128)S(1)}, ...), condition=%wide.region_3.4_spmd.clone.clone, body=%wide.region_0.0_spmd.clone.clone.sunk | while | flops 337266176 | bytes 4002620 | solution.py:57
  325.0 2.4 broadcast_multiply_fusion.2
  327.5 1.4 fusion.69
  331.3 1.3 fusion.67
  336.6 2.4 broadcast_multiply_fusion.2
  339.0 1.4 fusion.69
  348.2 2.4 broadcast_multiply_fusion.2
  350.6 1.4 fusion.69
  354.4 1.3 fusion.67
  359.7 2.4 broadcast_multiply_fusion.2
  362.1 1.4 fusion.69
  366.0 1.3 fusion.67
  371.3 2.4 broadcast_multiply_fusion.2
  373.7 1.4 fusion.69
  377.6 1.3 fusion.67
  382.8 2.4 broadcast_multiply_fusion.2
  385.2 1.4 fusion.69
  389.1 1.3 fusion.67
  394.4 2.4 broadcast_multiply_fusion.2
  396.8 1.4 fusion.69
  400.7 1.3 fusion.67
  405.9 2.4 broadcast_multiply_fusion.2
  408.3 1.4 fusion.69
  412.2 1.3 fusion.67
  417.5 2.4 broadcast_multiply_fusion.2
  419.9 1.4 fusion.69
  423.8 1.3 fusion.67
  429.0 2.4 broadcast_multiply_fusion.2
  431.5 1.4 fusion.69
  435.3 1.3 fusion.67
  440.6 2.4 broadcast_multiply_fusion.2
  443.0 1.4 fusion.69
  446.9 1.3 fusion.67
  452.1 2.4 broadcast_multiply_fusion.2
  454.6 1.4 fusion.69
  458.4 1.3 fusion.67
  463.7 2.4 broadcast_multiply_fusion.2
  466.1 1.4 fusion.69
  470.0 1.3 fusion.67
  475.2 2.4 broadcast_multiply_fusion.2
  477.7 1.4 fusion.69
  481.5 1.3 fusion.67
  486.8 2.4 broadcast_multiply_fusion.2
  489.2 1.4 fusion.69
  498.3 2.4 broadcast_multiply_fusion.2
  500.8 1.4 fusion.69
  508.1 2.1 reshape.454
  510.2 26.5 %all_to_all.32 = bf16[64,2,2048]{2,1,0:T(2,128)(2,1)S(1)} all-to-all(bf16[64,2,2048]{2,1,0:T(2,128)(2,1)S(1)} %reshape.454), channel_id=1, replica_groups=mesh['ctx'=64,'tp'=4] {'ctx'}, dimensions={0} | all-to-all | bytes 1048576 | tf_op jit(solution)/shard_map/all_to_all | solution.py:104
  536.7 7.1 %reshape.455 = bf16[8192,1,32]{2,1,0:T(2,128)(2,1)} reshape(bf16[64,2,2048]{2,1,0:T(2,128)(2,1)S(1)} %all_to_all.32) | data formatting | bytes 1048576
  543.9 8.0 %copy.70 = bf16[8192,1,32]{0,2,1:T(8,128)(2,1)S(1)} copy(bf16[8192,1,32]{2,1,0:T(2,128)(2,1)} %reshape.455) | data formatting | bytes 1048576 | tf_op jit(solution)/shard_map/all_to_all | solution.py:104
  554.1 9.6 %fusion.25 = f32[128,4096]{1,0:T(8,128)} fusion(bf16[1,2048,4096]{2,1,0:T(8,128)(2,1)} %all-gather.2.cloned.1.call-done, f32[128,1,2048]{0,2,1:T(8,128)S(1)} %get-tuple-element.142, f32[2048]{0:T(1024)S(1)} %bitcast.176, f32[128]{0:T(128)S(1)} %add_rsqrt_fusion), kind=kOutput, calls=%fused_computation.38 | convolution fusion | flops 2148270080 | bytes 19931648 | tf_op jit(solution)/shard_map/tgr,grd->td/dot_general | solution.py:111
  563.7 28.8 %reduce-scatter.2.cloned.1.call-done = f32[128,1024]{1,0:T(8,128)} async-done(((f32[128,4096]{1,0:T(8,128)}), f32[128,1024]{1,0:T(8,128)}) %reduce-scatter.2.cloned.1.call-update) | async-done | bytes 524304 | tf_op jit(solution)/shard_map/reduce_scatter | solution.py:117
  592.5 1.8 convert_element_type.107
  (251 shorter events, 101.0 us)
Async XLA Ops:
  6.5 77.7 %copy-start = (f32[1,32]{1,0:T(1,128)S(1)}, f32[1,32]{1,0:T(1,128)}, u32[]{:S(2)}) copy-start(f32[1,32]{1,0:T(1,128)} %param.13) | copy-start | bytes 388
  6.5 21.2 %copy-start.4 = (f32[1,4,2560]{2,1,0:T(4,128)S(1)}, f32[1,4,2560]{2,1,0:T(4,128)}, u32[]{:S(2)}) copy-start(f32[1,4,2560]{2,1,0:T(4,128)} %param.11) | copy-start | bytes 122884
  9.2 34.2 %all-to-all-start = ((bf16[128,1,64]{0,1,2:T(2,128)(2,1)}), bf16[128,1,64]{0,1,2:T(2,128)(2,1)S(1)}, u32[]{:S(2)}, u32[]{:S(2)}) async-start(bf16[128,1,64]{0,1,2:T(2,128)(2,1)} %copy.62), calls=%async_computation | async-start | bytes 65536 | tf_op jit(solution)/shard_map/all_to_all | solution.py:85
  22.4 5.5 slice-start
  24.0 4.1 copy-start.5
  24.0 4.6 collective-permute-start
  43.4 29.6 %all-to-all-start.1 = ((bf16[64,2,2048]{2,1,0:T(2,128)(2,1)}), bf16[64,2,2048]{2,1,0:T(2,128)(2,1)S(1)}, u32[]{:S(2)}, u32[]{:S(2)}) async-start(bf16[64,2,2048]{2,1,0:T(2,128)(2,1)} %reshape.452), calls=%async_computation.1 | async-start | bytes 1048576 | tf_op jit(solution)/shard_map/all_to_all | solution.py:84
  77.2 7.7 %copy-start.6 = (f32[1,32]{1,0:T(1,128)S(1)}, f32[1,32]{1,0:T(1,128)}, u32[]{:S(2)}) copy-start(f32[1,32]{1,0:T(1,128)} %param.14) | copy-start | bytes 388
  77.2 238.2 %all-to-all-start.2 = ((bf16[64,128,1,512]{3,1,2,0:T(8,128)(2,1)}), bf16[64,128,1,512]{3,1,2,0:T(8,128)(2,1)}, u32[]{:S(2)}, u32[]{:S(2)}) async-start(bf16[64,128,1,512]{3,1,2,0:T(8,128)(2,1)} %stack.2), calls=%async_computation.2 | async-start | bytes 16777216 | tf_op jit(solution)/shard_map/all_to_all | solution.py:88
  83.3 470.5 %all-gather.2.cloned.1.call-start = ((), (), s32[]{:S(2)}) async-start(), calls=%async_computation.5 | async-start | bytes 17039360 | tf_op jit(solution)/shard_map/all_gather | solution.py:114
  84.0 508.5 %reduce-scatter.2.cloned.1.call-start = ((), (), s32[]{:S(2)}) async-start(), calls=%async_computation.6 | async-start | bytes 2621440 | tf_op jit(solution)/shard_map/reduce_scatter | solution.py:117
  552.1 1.3 copy-start.2
  553.4 0.7 copy-start.3
  563.7 30.6 %copy-start.1 = (f32[1,32]{1,0:T(1,128)S(1)}, f32[1,32]{1,0:T(1,128)}, u32[]{:S(2)}) copy-start(f32[1,32]{1,0:T(1,128)} %param.13) | copy-start | bytes 388
Sparse Core Ops, SparseCore 0:
  86.9 222.1 all-gather.1
  563.8 28.6 reduce-scatter.1
